TPU v7x, 256 devices: a whole 4x4x8 slice. The times are simulated.
256 devices in a mesh: dp: 32 (over y, z), head: 8 (over x, core).
Axes of the slice: x: 4, y: 4, z: 8, core: 2. Of those that a mesh axis runs over, the one named last changes fastest.
Arguments:
- queries: bfloat16 [32768, 4096], P('dp', 'head'), may hold values from -6 to 6
- keys: bfloat16 [32768, 4096], P('dp', 'head'), may hold values from -6 to 6
- values: bfloat16 [32768, 4096], P('dp', 'head'), may hold values from -100 to 100
- out_grad: bfloat16 [32768, 4096], P('dp', 'head'), may hold values from -6 to 6
- norm_gain: float32 [4096], P('head'), may hold values from 0.1 to 1.9
- decay_table: float32 [16, 8], P('head'), may hold values from 0 to 0.52, as said below
- decay_index: int32 [16, 32768], P('head', 'dp'), may hold values from 0 to 7
- rollout_lengths: int32 [6], replicated, may hold values from 1 to 16384, 32768 in all
- move_partner: int32 [32], replicated, may hold values from 0 to 31, as said below
- move_slot: int32 [32], replicated, may hold values from 0 to 31, as said below
Outputs:
- query_grad: bfloat16 [32768, 4096], P('dp', 'head')
- key_grad: bfloat16 [32768, 4096], P('dp', 'head')
- value_grad: bfloat16 [32768, 4096], P('dp', 'head')
Inputs may be any that keep to these rules, and one draw needn't show every extreme that they name: `decay_table`: positive rates. `rollout_lengths`: they sum to 32768. move_partner[d] is either d itself or a row whose index differs from d in exactly one bit, and the partner of the partner is the row itself. `move_slot`: one block of each row.
All inputs are finite; a program needn't handle non-finite values.
Results may differ from a plain program's by a relative error of at most 0.0063.
Values may be sent and summed in bfloat16 or wider, within the bound.
No kernel may reach another device: no remote copies, remote signals or barrier semaphores. Data moves between devices by JAX's collectives and lax.ppermute only.
A program may use at most 128 MiB of HBM per device.

v0:
```python
import jax
import jax.numpy as jnp
from jax import lax
from jax.sharding import PartitionSpec as P

HEAD_DIM = 256
BLOCK_LEN = 32
FEATURES = 4096
EPSILON = 1e-05


def entering(part, axis, combine, identity, reverse):
    count = lax.axis_size(axis)
    place = lax.axis_index(axis)
    ahead = count - 1 - place if reverse else place
    gathered = jax.tree.map(lambda a: lax.all_gather(a, axis), part)
    state = jax.tree.map(lambda a, e: jnp.zeros_like(a) + jnp.asarray(e, a.dtype), part, identity)

    def one(turn, state):
        source = count - 1 - turn if reverse else turn
        return combine(
            state, jax.tree.map(lambda a: lax.dynamic_index_in_dim(a, source, 0, False), gathered)
        )

    return lax.fori_loop(0, ahead, one, state)


def edge_factors(rate, flag):
    segment = jnp.cumsum(flag.astype(jnp.int32))
    total = jnp.cumsum(rate, axis=1)
    first = jnp.where(segment[None, :] == 0, jnp.exp(-total), 0.0)
    last = jnp.where(segment[None, :] == segment[-1], jnp.exp(total - total[:, -1:]), 0.0)
    whole = jnp.where(segment[-1] == 0, jnp.exp(-total[:, -1]), 0.0)
    return (total, segment, first, last, whole)


def decay_matrix(total_row, segment):
    count = segment.shape[0]
    places = jnp.arange(count)
    inside = (segment[:, None] == segment[None, :]) & (places[:, None] >= places[None, :])
    return jnp.where(
        inside, jnp.exp(jnp.minimum(total_row[None, :] - total_row[:, None], 0.0)), 0.0
    )


def combine_states(before, behind):
    return (before[0] * behind[0], behind[0][:, None, None] * before[1] + behind[1])


def take_block(array, block_id, length, axis_dim):
    return lax.dynamic_slice_in_dim(array, block_id * length, length, axis_dim)


def place_block(array, block, block_id, axis_dim):
    return lax.dynamic_update_slice_in_dim(array, block, block_id * block.shape[axis_dim], axis_dim)


def contract_first(left, right):
    return lax.dot_general(
        left, right, (((0,), (0,)), ((), ())), preferred_element_type=jnp.float32
    )


def contract_last(left, right):
    return lax.dot_general(
        left, right, (((1,), (1,)), ((), ())), preferred_element_type=jnp.float32
    )


def local(
    queries,
    keys,
    values,
    out_grad,
    norm_gain,
    decay_table,
    decay_index,
    rollout_lengths,
    move_partner,
    move_slot,
):
    row_index = lax.axis_index("dp")
    row_tokens = queries.shape[0]
    heads_here = decay_table.shape[0]
    length = BLOCK_LEN
    partner = move_partner[row_index]
    own_slot = move_slot[row_index]
    outgoing = (
        take_block(queries, own_slot, length, 0),
        take_block(keys, own_slot, length, 0),
        take_block(values, own_slot, length, 0),
        take_block(out_grad, own_slot, length, 0),
        take_block(decay_index, own_slot, length, 1),
    )
    arrived = (
        lax.all_gather(outgoing[0], "dp", axis=0, tiled=True),
        lax.all_gather(outgoing[1], "dp", axis=0, tiled=True),
        lax.all_gather(outgoing[2], "dp", axis=0, tiled=True),
        lax.all_gather(outgoing[3], "dp", axis=0, tiled=True),
        lax.all_gather(outgoing[4], "dp", axis=1, tiled=True),
    )
    guest = tuple(
        (
            take_block(member, partner, length, axis_dim)
            for member, axis_dim in zip(arrived, (0, 0, 0, 0, 1))
        )
    )
    packed_q = place_block(queries, guest[0], own_slot, 0)
    packed_k = place_block(keys, guest[1], own_slot, 0)
    packed_v = place_block(values, guest[2], own_slot, 0)
    packed_dy = place_block(out_grad, guest[3], own_slot, 0)
    packed_index = place_block(decay_index, guest[4], own_slot, 1)
    level_ids = jnp.arange(decay_table.shape[1], dtype=jnp.int32)
    rate = jnp.sum(
        jnp.where(packed_index[:, :, None] == level_ids, decay_table[:, None, :], 0.0), axis=2
    )
    starts = jnp.cumsum(rollout_lengths) - rollout_lengths
    position = row_index * row_tokens + jnp.arange(row_tokens, dtype=jnp.int32)
    flag = jnp.any(position[:, None] == starts[None, :], axis=1)
    total, segment, first, last, whole = edge_factors(rate, flag)
    head_cols = []
    local_states = []
    for head_pos in range(heads_here):
        columns = slice(head_pos * HEAD_DIM, (head_pos + 1) * HEAD_DIM)
        head_cols.append(columns)
        gated_values = (packed_v[:, columns].astype(jnp.float32) * last[head_pos][:, None]).astype(
            jnp.bfloat16
        )
        local_states.append(contract_first(packed_k[:, columns], gated_values))
    stacked = jnp.stack(local_states)
    identity = (jnp.ones_like(whole), jnp.zeros_like(stacked))
    _, carry_in = entering((whole, stacked), "dp", combine_states, identity, False)
    carry_half = carry_in.astype(jnp.bfloat16)
    decays = []
    weight_list = []
    retained_parts = []
    for head_pos in range(heads_here):
        columns = head_cols[head_pos]
        query_head = packed_q[:, columns]
        decay = decay_matrix(total[head_pos], segment)
        scores = contract_last(query_head, packed_k[:, columns])
        weights = (scores * decay / HEAD_DIM).astype(jnp.bfloat16)
        inner_part = jnp.dot(weights, packed_v[:, columns], preferred_element_type=jnp.float32)
        cross_part = (
            first[head_pos][:, None]
            * jnp.dot(query_head, carry_half[head_pos], preferred_element_type=jnp.float32)
            / HEAD_DIM
        )
        decays.append(decay)
        weight_list.append(weights)
        retained_parts.append(inner_part + cross_part)
    retained = jnp.concatenate(retained_parts, axis=1)
    scaled = norm_gain * packed_dy.astype(jnp.float32)
    squares, inner = lax.psum(
        (jnp.sum(retained * retained, axis=1), jnp.sum(scaled * retained, axis=1)), "head"
    )
    recip = lax.rsqrt(squares / FEATURES + EPSILON)
    norm_grad = (
        recip[:, None] * scaled - (recip**3 * inner / FEATURES)[:, None] * retained
    ).astype(jnp.bfloat16)
    back_locals = []
    for head_pos in range(heads_here):
        columns = head_cols[head_pos]
        weighted = (norm_grad[:, columns].astype(jnp.float32) * first[head_pos][:, None]).astype(
            jnp.bfloat16
        )
        back_locals.append(contract_first(packed_q[:, columns], weighted) / HEAD_DIM)
    back_stack = jnp.stack(back_locals)
    _, carry_back = entering(
        (whole, back_stack),
        "dp",
        combine_states,
        (jnp.ones_like(whole), jnp.zeros_like(back_stack)),
        True,
    )
    back_half = carry_back.astype(jnp.bfloat16)
    query_parts = []
    key_parts = []
    value_parts = []
    for head_pos in range(heads_here):
        columns = head_cols[head_pos]
        query_head = packed_q[:, columns]
        key_head = packed_k[:, columns]
        value_head = packed_v[:, columns]
        grad_head = norm_grad[:, columns]
        grad_scores = contract_last(grad_head, value_head)
        grad_weights = (grad_scores * decays[head_pos] / HEAD_DIM).astype(jnp.bfloat16)
        query_part = jnp.dot(grad_weights, key_head, preferred_element_type=jnp.float32)
        query_part = (
            query_part
            + first[head_pos][:, None] * contract_last(grad_head, carry_half[head_pos]) / HEAD_DIM
        )
        key_part = contract_first(grad_weights, query_head)
        key_part = key_part + last[head_pos][:, None] * contract_last(
            value_head, back_half[head_pos]
        )
        value_part = contract_first(weight_list[head_pos], grad_head)
        value_part = value_part + last[head_pos][:, None] * jnp.dot(
            key_head, back_half[head_pos], preferred_element_type=jnp.float32
        )
        query_parts.append(query_part)
        key_parts.append(key_part)
        value_parts.append(value_part)
    packed_grads = (
        jnp.concatenate(query_parts, axis=1).astype(jnp.bfloat16),
        jnp.concatenate(key_parts, axis=1).astype(jnp.bfloat16),
        jnp.concatenate(value_parts, axis=1).astype(jnp.bfloat16),
    )
    leaving = tuple((take_block(member, own_slot, length, 0) for member in packed_grads))
    returned_all = (
        lax.all_gather(leaving[0], "dp", axis=0, tiled=True),
        lax.all_gather(leaving[1], "dp", axis=0, tiled=True),
        lax.all_gather(leaving[2], "dp", axis=0, tiled=True),
    )
    returned = tuple((take_block(member, partner, length, 0) for member in returned_all))
    query_grad = place_block(packed_grads[0], returned[0], own_slot, 0)
    key_grad = place_block(packed_grads[1], returned[1], own_slot, 0)
    value_grad = place_block(packed_grads[2], returned[2], own_slot, 0)
    return (query_grad, key_grad, value_grad)


def solution(mesh):
    placed = (
        P("dp", "head"),
        P("dp", "head"),
        P("dp", "head"),
        P("dp", "head"),
        P("head"),
        P("head", None),
        P("head", "dp"),
        P(),
        P(),
        P(),
    )
    return jax.shard_map(
        local,
        mesh=mesh,
        in_specs=placed,
        out_specs=(P("dp", "head"), P("dp", "head"), P("dp", "head")),
        check_vma=False,
    )
```

profile of v0, /device:TPU:2, one launch (start us, length us, event | category | flops | bytes accessed | tf_op | source)
XLA Modules:
  0.0 900.6 jit_solution(8727087491861123065)
XLA Ops:
  7.3 1.2 copy.103
  8.5 1.2 copy.102
  11.0 1.4 constant_dynamic-slice_fusion.6
  13.2 1.4 constant_dynamic-slice_fusion.4
  16.6 1.5 copy.47
  19.7 46.3 %all-gather.3 = s32[32,32,2]{1,2,0:T(2,128)S(1)} all-gather(s32[1,32,2]{1,2,0:T(2,128)S(1)} %fusion.70), channel_id=1, replica_groups=mesh['dp'=32,'head'=8] {'dp'}, dimensions={0}, use_global_device_ids=true | all-gather | bytes 8448 | tf_op jit(solution)/shard_map/all_gather | solution.py:100
  68.4 23.5 %all-gather.18.cloned.1.call-done = bf16[1024,512]{1,0:T(8,128)(2,1)} async-done(((bf16[32,512]{1,0:T(8,128)(2,1)}), bf16[1024,512]{1,0:T(8,128)(2,1)}) %all-gather.18.cloned.1.call-update) | async-done | bytes 1048592 | tf_op jit(solution)/shard_map/all_gather | solution.py:98
  93.7 74.8 %all-gather.16.cloned.1.call-done = bf16[1024,512]{1,0:T(8,128)(2,1)} async-done(((bf16[32,512]{1,0:T(8,128)(2,1)}), bf16[1024,512]{1,0:T(8,128)(2,1)}) %all-gather.16.cloned.1.call-update) | async-done | bytes 1048592 | tf_op jit(solution)/shard_map/all_gather | solution.py:97
  171.5 1.5 copy.50
  174.4 72.2 %all-reduce = f32[64]{0:T(128)S(1)} all-reduce(f32[64]{0:T(128)S(1)} %fusion.73), channel_id=2, replica_groups=mesh['dp'=32,'head'=8] {'dp'}, use_global_device_ids=true, to_apply=%add | all-reduce | flops 64 | bytes 512
  248.6 73.8 %all-gather.14.cloned.1.call-done = bf16[1024,512]{1,0:T(8,128)(2,1)} async-done(((bf16[32,512]{1,0:T(8,128)(2,1)}), bf16[1024,512]{1,0:T(8,128)(2,1)}) %all-gather.14.cloned.1.call-update) | async-done | bytes 1048592 | tf_op jit(solution)/shard_map/all_gather | solution.py:96
  323.2 2.1 multiply_convert_fusion.2
  325.3 1.7 fusion.42
  327.1 2.1 multiply_convert_fusion.3
  329.2 1.3 copy-done.13
  330.5 1.8 fusion.53
  332.3 129.7 %all-gather.28.cloned.1.call-done = f32[64,256,256]{2,1,0:T(8,128)} async-done(((f32[2,256,256]{2,1,0:T(8,128)}), f32[64,256,256]{2,1,0:T(8,128)}) %all-gather.28.cloned.1.call-update) | async-done | bytes 16777232 | tf_op jit(solution)/shard_map/all_gather | solution.py:16
  462.1 1.8 fusion.10
  463.9 1.8 fusion.12
  466.7 11.1 %all-reduce.1 = (f32[1024]{0:T(1024)S(1)}, f32[1024]{0:T(1024)S(1)}) all-reduce(f32[1024]{0:T(1024)S(1)} %get-tuple-element.146, f32[1024]{0:T(1024)S(1)} %get-tuple-element.145), channel_id=1, replica_groups=mesh['dp'=32,'head'=8] {'head'}, use_global_device_ids=true, to_apply=%region_12.13 | all-reduce | flops 2048 | bytes 16384 | tf_op jit(solution)/shard_map/psum | solution.py:154
  477.8 2.0 subtract_convert_fusion
  479.8 1.5 fusion.20
  481.3 1.4 fusion.19
  483.8 2.3 multiply_convert_fusion
  488.1 2.2 multiply_convert_fusion.1
  493.4 3.3 fusion.32
  496.7 3.3 fusion.27
  500.0 157.3 %all-gather.30.cloned.1.call-done = f32[64,256,256]{2,1,0:T(8,128)} async-done(((f32[2,256,256]{2,1,0:T(8,128)}), f32[64,256,256]{2,1,0:T(8,128)}) %all-gather.30.cloned.1.call-update) | async-done | bytes 16777232 | tf_op jit(solution)/shard_map/all_gather | solution.py:16
  657.3 38.7 %while.27 = (s32[]{:T(128)}, f32[2,256,256]{2,1,0:T(8,128)S(1)}, s32[]{:T(128)}, f32[32,2]{1,0:T(8,128)S(1)}, f32[32,2,256,256]{3,2,1,0:T(8,128)}, /*index=5*/s32[]{:T(128)}, s32[]{:T(128)}, s32[]{:T(128)}, s32[]{:T(128)}) while((s32[]{:T(128)}, f32[2,256,256]{2,1,0:T(8,128)S(1)}, s32[]{:T(128)}, f32[32,2]{1,0:T(8,128)S(1)}, ...), condition=%wide.region_14.15_spmd, body=%wide.region_13.14_spmd.sunk | while | flops 262150 | bytes 1573043 | solution.py:25
  657.4 1.3 bitcast_add_fusion.5
  660.0 1.2 bitcast_add_fusion.5
  661.2 1.2 bitcast_add_fusion.5
  666.2 1.2 bitcast_add_fusion.5
  668.7 1.2 bitcast_add_fusion.5
  674.9 1.2 bitcast_add_fusion.5
  682.4 1.2 bitcast_add_fusion.5
  686.1 1.2 bitcast_add_fusion.5
  691.1 1.2 bitcast_add_fusion.5
  696.5 1.6 fusion.13
  699.0 2.6 fusion.35
  704.9 28.5 %all-gather.22.cloned.1.call-done = bf16[1024,512]{1,0:T(8,128)(2,1)} async-done(((bf16[32,512]{1,0:T(8,128)(2,1)}), bf16[1024,512]{1,0:T(8,128)(2,1)}) %all-gather.22.cloned.1.call-update) | async-done | bytes 1048592 | tf_op jit(solution)/shard_map/all_gather | solution.py:211
  734.3 2.2 dynamic_update_slice.31
  736.5 2.3 copy.57
  739.9 70.0 %all-gather.26.cloned.1.call-done = bf16[1024,512]{1,0:T(8,128)(2,1)} async-done(((bf16[32,512]{1,0:T(8,128)(2,1)}), bf16[1024,512]{1,0:T(8,128)(2,1)}) %all-gather.26.cloned.1.call-update) | async-done | bytes 1048592 | tf_op jit(solution)/shard_map/all_gather | solution.py:213
  809.9 76.5 %all-gather.24.cloned.1.call-done = bf16[1024,512]{1,0:T(8,128)(2,1)} async-done(((bf16[32,512]{1,0:T(8,128)(2,1)}), bf16[1024,512]{1,0:T(8,128)(2,1)}) %all-gather.24.cloned.1.call-update) | async-done | bytes 1048592 | tf_op jit(solution)/shard_map/all_gather | solution.py:212
  887.3 2.2 dynamic_update_slice.33
  889.4 2.3 copy.59
  892.8 1.3 copy.58
  (203 shorter events, 56.9 us)
Async XLA Ops:
  7.2 59.2 %copy-start.20 = (f32[2,8]{1,0:T(2,128)S(1)}, f32[2,8]{1,0:T(2,128)}, u32[]{:S(2)}) copy-start(f32[2,8]{1,0:T(2,128)} %param.19) | copy-start | bytes 196
  7.2 2.5 copy-start.18
  7.2 10.9 %copy-start.23 = (s32[6]{0:T(128)S(1)}, s32[6]{0:T(128)}, u32[]{:S(2)}) copy-start(s32[6]{0:T(128)} %param.21) | copy-start | bytes 76
  7.2 8.1 copy-start.22
  7.2 2.5 copy-start.21
  7.2 84.7 %all-gather.18.cloned.1.call-start = ((), (), s32[]{:S(2)}) async-start(), calls=%async_computation.2 | async-start | bytes 1081344 | tf_op jit(solution)/shard_map/all_gather | solution.py:98
  12.4 156.1 %all-gather.16.cloned.1.call-start = ((), (), s32[]{:S(2)}) async-start(), calls=%async_computation.1 | async-start | bytes 1081344 | tf_op jit(solution)/shard_map/all_gather | solution.py:97
  13.1 233.6 %all-gather.20.cloned.1.call-start = ((), (), s32[]{:S(2)}) async-start(), calls=%async_computation.3 | async-start | bytes 1081344 | tf_op jit(solution)/shard_map/all_gather | solution.py:99
  14.6 307.8 %all-gather.14.cloned.1.call-start = ((), (), s32[]{:S(2)}) async-start(), calls=%async_computation | async-start | bytes 1081344 | tf_op jit(solution)/shard_map/all_gather | solution.py:96
  15.3 446.7 %all-gather.28.cloned.1.call-start = ((), (), s32[]{:S(2)}) async-start(), calls=%async_computation.7 | async-start | bytes 17301504 | tf_op jit(solution)/shard_map/all_gather | solution.py:16
  18.1 154.9 %copy-start.24 = (u32[256]{0:T(256)S(1)}, u32[256]{0:T(256)}, u32[]{:S(2)}) copy-start(u32[256]{0:T(256)} %constant.107) | copy-start | bytes 3076
  93.7 77.2 %copy-start.6 = (bf16[1024,512]{0,1:T(8,128)(2,1)}, bf16[1024,512]{0,1:T(8,128)(2,1)S(1)}, u32[]{:S(2)}) copy-start(bf16[1024,512]{0,1:T(8,128)(2,1)S(1)} %dynamic_update_slice.29) | copy-start | bytes 3145732
  170.8 486.5 %all-gather.30.cloned.1.call-start = ((), (), s32[]{:S(2)}) async-start(), calls=%async_computation.8 | async-start | bytes 17301504 | tf_op jit(solution)/shard_map/all_gather | solution.py:16
  323.2 3.9 copy-start.4
  323.2 2.2 copy-start.7
  325.3 3.9 copy-start.12
  329.2 1.3 copy-start.13
  462.0 1.9 copy-start.17
  462.0 3.7 copy-start.19
  463.9 1.8 copy-start
  465.7 1.0 copy-start.1
  479.8 4.0 copy-start.8
  483.6 249.9 %all-gather.22.cloned.1.call-start = ((), (), s32[]{:S(2)}) async-start(), calls=%async_computation.4 | async-start | bytes 1081344 | tf_op jit(solution)/shard_map/all_gather | solution.py:211
  486.1 4.2 copy-start.14
  486.1 2.0 copy-start.9
  490.3 1.4 copy-start.15
  491.7 0.9 copy-start.2
  500.0 309.9 %all-gather.26.cloned.1.call-start = ((), (), s32[]{:S(2)}) async-start(), calls=%async_computation.6 | async-start | bytes 1081344 | tf_op jit(solution)/shard_map/all_gather | solution.py:213
  657.3 38.8 %copy-start.11 = (f32[1024,256]{0,1:T(8,128)S(1)}, f32[1024,256]{0,1:T(8,128)}, u32[]{:S(2)}) copy-start(f32[1024,256]{0,1:T(8,128)} %fusion.27) | copy-start | bytes 3145732
  698.1 3.5 copy-start.5
  698.9 187.4 %all-gather.24.cloned.1.call-start = ((), (), s32[]{:S(2)}) async-start(), calls=%async_computation.5 | async-start | bytes 1081344 | tf_op jit(solution)/shard_map/all_gather | solution.py:212
  699.0 2.6 copy-start.16
  699.0 3.4 copy-start.10
  702.4 1.5 copy-start.3
Sparse Core Ops, SparseCore 0:
  12.5 79.3 all-gather.17
  94.5 73.9 all-gather.15
  171.6 73.8 all-gather.19
  248.5 73.8 all-gather.13
  324.8 137.1 all-gather.27
  483.7 173.5 all-gather.29
  659.9 73.4 all-gather.21
  736.0 73.8 all-gather.25
  812.5 73.8 all-gather.23
where the time goes:
time: 903 us; the launch traced here: 901 us
  waiting for transfers between devices  634 us (70%)
  blocking collectives  130 us (14%)
  other arithmetic  46.7 us (5%)
  local copies, waits for them, and re-layouts  37.5 us (4%)
  matrix products  34 us (4%)
  between operations  17.1 us (2%)
    all_gather x2, waiting for transfers between devices, entering(): gathered = jax.tree.map(lambda a: lax.all_gather(a, axis), part)  287 us
    all_gather x1, waiting for transfers between devices, local(): lax.all_gather(leaving[1], 'dp', axis=0, tiled=True)  76.5 us
    all_gather x1, waiting for transfers between devices, local(): lax.all_gather(outgoing[1], 'dp', axis=0, tiled=True)  74.8 us
    all_gather x1, waiting for transfers between devices, local(): lax.all_gather(outgoing[0], 'dp', axis=0, tiled=True)  73.8 us
    unnamed x1, blocking collectives  72.2 us
    all_gather x1, waiting for transfers between devices, local(): lax.all_gather(leaving[2], 'dp', axis=0, tiled=True)  70 us
    all_gather x1, blocking collectives, local(): lax.all_gather(outgoing[4], 'dp', axis=1, tiled=True)  46.3 us
    add x31, other arithmetic, combine_states(): behind[0][:, None, None] * before[1] + behind[1]  37.5 us
  transfers between devices with their start and end apart: 9, of which 8 were waited for; matrix products, arithmetic and copies ran while one was open for 10% of the time, Pallas kernels for 0%

commit v1 on v0

--- a/solution.py
+++ b/solution.py
@@ -7,6 +7,13 @@
 BLOCK_LEN = 32
 FEATURES = 4096
 EPSILON = 1e-05
+
+
+def gather_over(x, axis, d):
+    size = lax.axis_size(axis)
+    shards = jnp.stack([x for _ in range(size)])
+    shards = lax.all_to_all(shards, axis, split_axis=0, concat_axis=0)
+    return jnp.concatenate(shards, axis=d)
 
 
 def entering(part, axis, combine, identity, reverse):
@@ -93,7 +100,7 @@
         take_block(decay_index, own_slot, length, 1),
     )
     arrived = (
-        lax.all_gather(outgoing[0], "dp", axis=0, tiled=True),
+        gather_over(outgoing[0], "dp", 0),
         lax.all_gather(outgoing[1], "dp", axis=0, tiled=True),
         lax.all_gather(outgoing[2], "dp", axis=0, tiled=True),
         lax.all_gather(outgoing[3], "dp", axis=0, tiled=True),

time: 903 us -> 829 us (0.918)
  waiting for transfers between devices: 634 us -> 541 us
  blocking collectives: 130 us -> 141 us
    all_gather x1 -> x0, waiting for transfers between devices: 73.8 us -> none  [local(): lax.all_gather(outgoing[0], 'dp', axis=0, tiled=True)]
    all_gather x2, waiting for transfers between devices: 287 us -> 266 us  [entering(): gathered = jax.tree.map(lambda a: lax.all_gather(a, axis), part)]
    unnamed x1, blocking collectives: 72.2 us -> 83.3 us
  transfers between devices with their start and end apart: 9 -> 9, of which waited for: 8 -> 7; matrix products, arithmetic and copies ran while one was open for 10% -> 11% of each run, Pallas kernels for 0% -> 0%
where the time goes in v1:
time: 829 us; the launch traced here: 826 us
  waiting for transfers between devices  541 us (65%)
  blocking collectives  141 us (17%)
  other arithmetic  46.7 us (6%)
  local copies, waits for them, and re-layouts  38.6 us (5%)
  matrix products  34 us (4%)
  between operations  17.3 us (2%)
    all_gather x2, waiting for transfers between devices, entering(): gathered = jax.tree.map(lambda a: lax.all_gather(a, axis), part)  266 us
    unnamed x1, blocking collectives  83.3 us
    all_gather x1, waiting for transfers between devices, local(): lax.all_gather(leaving[1], 'dp', axis=0, tiled=True)  76.5 us
    all_gather x1, waiting for transfers between devices, local(): lax.all_gather(outgoing[1], 'dp', axis=0, tiled=True)  75.3 us
    all_gather x1, waiting for transfers between devices, local(): lax.all_gather(leaving[2], 'dp', axis=0, tiled=True)  70 us
    all_gather x1, blocking collectives, local(): lax.all_gather(outgoing[4], 'dp', axis=1, tiled=True)  46.3 us
    add x31, other arithmetic, combine_states(): behind[0][:, None, None] * before[1] + behind[1]  37.5 us
    all_gather x1, waiting for transfers between devices, local(): lax.all_gather(leaving[0], 'dp', axis=0, tiled=True)  28.4 us
  transfers between devices with their start and end apart: 9, of which 7 were waited for; matrix products, arithmetic and copies ran while one was open for 11% of the time, Pallas kernels for 0%

profile of v1, /device:TPU:2, one launch (start us, length us, event | category | flops | bytes accessed | tf_op | source)
XLA Modules:
  0.0 825.8 jit_solution(2661427984109557643)
XLA Ops:
  7.3 1.2 copy.103
  9.2 1.2 copy.102
  11.6 1.4 constant_dynamic-slice_fusion.6
  13.8 1.4 constant_dynamic-slice_fusion.4
  16.4 1.5 copy.47
  19.5 46.3 %all-gather.3 = s32[32,32,2]{1,2,0:T(2,128)S(1)} all-gather(s32[1,32,2]{1,2,0:T(2,128)S(1)} %fusion.70), channel_id=1, replica_groups=mesh['dp'=32,'head'=8] {'dp'}, dimensions={0}, use_global_device_ids=true | all-gather | bytes 8448 | tf_op jit(solution)/shard_map/all_gather | solution.py:107
  68.2 24.2 %all-gather.15.cloned.1.call-done = bf16[1024,512]{1,0:T(8,128)(2,1)} async-done(((bf16[32,512]{1,0:T(8,128)(2,1)}), bf16[1024,512]{1,0:T(8,128)(2,1)}) %all-gather.15.cloned.1.call-update) | async-done | bytes 1048592 | tf_op jit(solution)/shard_map/all_gather | solution.py:105
  94.3 75.3 %all-gather.13.cloned.1.call-done = bf16[1024,512]{1,0:T(8,128)(2,1)} async-done(((bf16[32,512]{1,0:T(8,128)(2,1)}), bf16[1024,512]{1,0:T(8,128)(2,1)}) %all-gather.13.cloned.1.call-update) | async-done | bytes 1048592 | tf_op jit(solution)/shard_map/all_gather | solution.py:104
  173.1 6.1 all-to-all-start
  179.9 1.5 copy.50
  182.7 83.3 %all-reduce = f32[64]{0:T(128)S(1)} all-reduce(f32[64]{0:T(128)S(1)} %fusion.73), channel_id=2, replica_groups=mesh['dp'=32,'head'=8] {'dp'}, use_global_device_ids=true, to_apply=%add | all-reduce | flops 64 | bytes 512
  268.8 2.1 multiply_convert_fusion.2
  271.0 1.7 fusion.42
  272.7 2.1 multiply_convert_fusion.3
  274.9 1.3 copy-done.13
  276.2 1.7 fusion.53
  278.0 108.8 %all-gather.25.cloned.1.call-done = f32[64,256,256]{2,1,0:T(8,128)} async-done(((f32[2,256,256]{2,1,0:T(8,128)}), f32[64,256,256]{2,1,0:T(8,128)}) %all-gather.25.cloned.1.call-update) | async-done | bytes 16777232 | tf_op jit(solution)/shard_map/all_gather | solution.py:23
  386.8 1.8 fusion.10
  388.7 1.8 fusion.12
  391.5 11.1 %all-reduce.1 = (f32[1024]{0:T(1024)S(1)}, f32[1024]{0:T(1024)S(1)}) all-reduce(f32[1024]{0:T(1024)S(1)} %get-tuple-element.146, f32[1024]{0:T(1024)S(1)} %get-tuple-element.145), channel_id=1, replica_groups=mesh['dp'=32,'head'=8] {'head'}, use_global_device_ids=true, to_apply=%region_12.13 | all-reduce | flops 2048 | bytes 16384 | tf_op jit(solution)/shard_map/psum | solution.py:161
  402.6 2.0 subtract_convert_fusion
  404.6 1.5 fusion.20
  406.0 1.4 fusion.19
  408.6 2.3 multiply_convert_fusion
  412.8 2.2 multiply_convert_fusion.1
  418.1 3.3 fusion.32
  421.4 3.3 fusion.27
  424.7 157.6 %all-gather.27.cloned.1.call-done = f32[64,256,256]{2,1,0:T(8,128)} async-done(((f32[2,256,256]{2,1,0:T(8,128)}), f32[64,256,256]{2,1,0:T(8,128)}) %all-gather.27.cloned.1.call-update) | async-done | bytes 16777232 | tf_op jit(solution)/shard_map/all_gather | solution.py:23
  582.4 38.7 %while.27 = (s32[]{:T(128)}, f32[2,256,256]{2,1,0:T(8,128)S(1)}, s32[]{:T(128)}, f32[32,2]{1,0:T(8,128)S(1)}, f32[32,2,256,256]{3,2,1,0:T(8,128)}, /*index=5*/s32[]{:T(128)}, s32[]{:T(128)}, s32[]{:T(128)}, s32[]{:T(128)}) while((s32[]{:T(128)}, f32[2,256,256]{2,1,0:T(8,128)S(1)}, s32[]{:T(128)}, f32[32,2]{1,0:T(8,128)S(1)}, ...), condition=%wide.region_14.15_spmd, body=%wide.region_13.14_spmd.sunk | while | flops 262150 | bytes 1573043 | solution.py:32
  582.4 1.3 bitcast_add_fusion.5
  583.8 1.2 bitcast_add_fusion.5
  585.0 1.2 bitcast_add_fusion.5
  588.8 1.2 bitcast_add_fusion.5
  590.0 1.2 bitcast_add_fusion.5
  593.7 1.2 bitcast_add_fusion.5
  600.0 1.2 bitcast_add_fusion.5
  607.5 1.2 bitcast_add_fusion.5
  611.2 1.2 bitcast_add_fusion.5
  621.5 1.6 fusion.13
  624.1 2.6 fusion.35
  630.0 28.4 %all-gather.19.cloned.1.call-done = bf16[1024,512]{1,0:T(8,128)(2,1)} async-done(((bf16[32,512]{1,0:T(8,128)(2,1)}), bf16[1024,512]{1,0:T(8,128)(2,1)}) %all-gather.19.cloned.1.call-update) | async-done | bytes 1048592 | tf_op jit(solution)/shard_map/all_gather | solution.py:218
  659.2 2.2 dynamic_update_slice.31
  661.4 2.3 copy.57
  664.8 70.0 %all-gather.23.cloned.1.call-done = bf16[1024,512]{1,0:T(8,128)(2,1)} async-done(((bf16[32,512]{1,0:T(8,128)(2,1)}), bf16[1024,512]{1,0:T(8,128)(2,1)}) %all-gather.23.cloned.1.call-update) | async-done | bytes 1048592 | tf_op jit(solution)/shard_map/all_gather | solution.py:220
  734.8 76.5 %all-gather.21.cloned.1.call-done = bf16[1024,512]{1,0:T(8,128)(2,1)} async-done(((bf16[32,512]{1,0:T(8,128)(2,1)}), bf16[1024,512]{1,0:T(8,128)(2,1)}) %all-gather.21.cloned.1.call-update) | async-done | bytes 1048592 | tf_op jit(solution)/shard_map/all_gather | solution.py:219
  812.2 2.2 dynamic_update_slice.33
  814.3 2.3 copy.59
  817.7 1.3 copy.58
  (201 shorter events, 58.0 us)
Async XLA Ops:
  7.2 59.0 %copy-start.19 = (f32[2,8]{1,0:T(2,128)S(1)}, f32[2,8]{1,0:T(2,128)}, u32[]{:S(2)}) copy-start(f32[2,8]{1,0:T(2,128)} %param.19) | copy-start | bytes 196
  7.2 10.8 %copy-start.22 = (s32[6]{0:T(128)S(1)}, s32[6]{0:T(128)}, u32[]{:S(2)}) copy-start(s32[6]{0:T(128)} %param.21) | copy-start | bytes 76
  7.2 8.1 copy-start.21
  7.2 3.2 copy-start.20
  7.2 85.3 %all-gather.15.cloned.1.call-start = ((), (), s32[]{:S(2)}) async-start(), calls=%async_computation.2 | async-start | bytes 1081344 | tf_op jit(solution)/shard_map/all_gather | solution.py:105
  13.0 156.6 %all-gather.13.cloned.1.call-start = ((), (), s32[]{:S(2)}) async-start(), calls=%async_computation.1 | async-start | bytes 1081344 | tf_op jit(solution)/shard_map/all_gather | solution.py:104
  13.8 252.4 %all-gather.17.cloned.1.call-start = ((), (), s32[]{:S(2)}) async-start(), calls=%async_computation.3 | async-start | bytes 1081344 | tf_op jit(solution)/shard_map/all_gather | solution.py:106
  15.3 371.4 %all-gather.25.cloned.1.call-start = ((), (), s32[]{:S(2)}) async-start(), calls=%async_computation.7 | async-start | bytes 17301504 | tf_op jit(solution)/shard_map/all_gather | solution.py:23
  94.3 78.8 %copy-start.6 = (bf16[1024,512]{0,1:T(8,128)(2,1)}, bf16[1024,512]{0,1:T(8,128)(2,1)S(1)}, u32[]{:S(2)}) copy-start(bf16[1024,512]{0,1:T(8,128)(2,1)S(1)} %dynamic_update_slice.29) | copy-start | bytes 3145732
  170.7 10.7 %copy-start.23 = (u32[256]{0:T(256)S(1)}, u32[256]{0:T(256)}, u32[]{:S(2)}) copy-start(u32[256]{0:T(256)} %constant.107) | copy-start | bytes 3076
  173.1 95.0 %all-to-all-start = ((bf16[32,32,512]{2,1,0:T(8,128)(2,1)}), bf16[32,32,512]{2,1,0:T(8,128)(2,1)}, u32[]{:S(2)}, u32[]{:S(2)}) async-start(bf16[32,32,512]{2,1,0:T(8,128)(2,1)} %stack.14), calls=%async_computation | async-start | bytes 2097152 | tf_op jit(solution)/shard_map/all_to_all | solution.py:15
  179.2 403.2 %all-gather.27.cloned.1.call-start = ((), (), s32[]{:S(2)}) async-start(), calls=%async_computation.8 | async-start | bytes 17301504 | tf_op jit(solution)/shard_map/all_gather | solution.py:23
  268.8 3.9 copy-start.4
  268.8 2.2 copy-start.7
  271.0 3.9 copy-start.12
  274.9 1.3 copy-start.13
  386.8 1.9 copy-start.17
  386.8 3.7 copy-start.18
  388.6 1.8 copy-start
  390.5 1.0 copy-start.1
  404.5 4.0 copy-start.8
  408.3 250.0 %all-gather.19.cloned.1.call-start = ((), (), s32[]{:S(2)}) async-start(), calls=%async_computation.4 | async-start | bytes 1081344 | tf_op jit(solution)/shard_map/all_gather | solution.py:218
  410.8 4.2 copy-start.14
  410.8 2.0 copy-start.9
  415.1 1.4 copy-start.15
  416.4 0.9 copy-start.2
  424.7 310.1 %all-gather.23.cloned.1.call-start = ((), (), s32[]{:S(2)}) async-start(), calls=%async_computation.6 | async-start | bytes 1081344 | tf_op jit(solution)/shard_map/all_gather | solution.py:220
  582.4 38.8 %copy-start.11 = (f32[1024,256]{0,1:T(8,128)S(1)}, f32[1024,256]{0,1:T(8,128)}, u32[]{:S(2)}) copy-start(f32[1024,256]{0,1:T(8,128)} %fusion.27) | copy-start | bytes 3145732
  623.1 3.5 copy-start.5
  624.0 187.3 %all-gather.21.cloned.1.call-start = ((), (), s32[]{:S(2)}) async-start(), calls=%async_computation.5 | async-start | bytes 1081344 | tf_op jit(solution)/shard_map/all_gather | solution.py:219
  624.0 2.6 copy-start.16
  624.0 3.4 copy-start.10
  627.4 1.5 copy-start.3
Sparse Core Ops, SparseCore 0:
  13.2 79.2 all-gather.14
  95.6 73.9 all-gather.12
  172.8 74.2 all-gather.16
  249.5 137.1 all-gather.24
  408.4 173.8 all-gather.26
  584.8 73.5 all-gather.18
  660.9 73.8 all-gather.22
  737.4 73.8 all-gather.20
